TPU v7x, 256 devices: a whole 4x4x8 slice. The times are simulated.
256 devices in a mesh: ctx: 16 (over z, core), ch: 16 (over x, y).
Axes of the slice: x: 4, y: 4, z: 8, core: 2. Of those that a mesh axis runs over, the one named last changes fastest.
Arguments:
- layer_input: bfloat16 [6144, 16384], P('ctx', 'ch'), may hold values from -6 to 6
- gate_input: bfloat16 [6144, 16384], P('ctx', 'ch'), may hold values from -6 to 6
- conv_weight: float32 [4, 16384], P(None, 'ch'), may hold values from -3 to 3
- conv_bias: float32 [16384], P('ch'), may hold values from -3 to 3
- select_weight: bfloat16 [544, 16384], P(None, 'ch'), may hold values from -0.046875 to 0.046875
- step_weight: bfloat16 [512, 16384], P(None, 'ch'), may hold values from -0.25 to 0.25
- step_bias: float32 [16384], P('ch')
- decay_log: float32 [16, 16384], P(None, 'ch')
- skip_gain: float32 [16384], P('ch'), may hold values from 0.5 to 1.5
- out_weight: bfloat16 [16384, 4096], P('ch'), may hold values from -0.046875 to 0.046875
- residual: bfloat16 [6144, 4096], P('ctx', 'ch')
- norm_gain: float32 [4096], replicated, may hold values from 0.5 to 1.5
- head_weight: bfloat16 [4096, 32768], P('ctx', 'ch')
- targets: int32 [6144], P('ctx'), may hold values from 0 to 32767
Outputs:
- token_logprob: float32 [6144], P('ctx')
- mean_logprob: float32 [6144], P('ctx')
- logprob_variance: float32 [6144], P('ctx')
All inputs are finite; a program needn't handle non-finite values.
Results may differ from a plain program's by a relative error of at most 0.0051.
Values may be sent and summed in bfloat16 or wider, within the bound.
A program may use at most 128 MiB of HBM per device.

v0:
```python
import jax
import jax.numpy as jnp
from jax import lax
from jax.sharding import PartitionSpec as P

STATE = 16
RANK = 512
KCONV = 4


def from_behind(shard, axis, by):
    size = lax.axis_size(axis)
    pairs = [(i, i + by) for i in range(size) if 0 <= i + by < size]
    return lax.ppermute(shard, axis, pairs)


def sigmoid_linear(operand):
    return operand / (1.0 + jnp.exp(-operand))


def smooth_relu(operand):
    return jnp.logaddexp(operand, 0.0)


def per_device(
    layer_input,
    gate_input,
    conv_weight,
    conv_bias,
    select_weight,
    step_weight,
    step_bias,
    decay_log,
    skip_gain,
    out_weight,
    residual,
    norm_gain,
    head_weight,
    targets,
):
    tok_rows, channels = layer_input.shape
    edge_rows = from_behind(layer_input[tok_rows - (KCONV - 1) :], "ctx", 1)
    padded = jnp.concatenate([edge_rows, layer_input], axis=0).astype(jnp.float32)
    convolved = jnp.zeros((tok_rows, channels), jnp.float32) + conv_bias[None, :]
    for offset in range(KCONV):
        convolved = convolved + conv_weight[offset][None, :] * padded[offset : offset + tok_rows]
    smoothed = sigmoid_linear(convolved).astype(jnp.bfloat16)
    partial_sums = lax.dot_general(
        select_weight, smoothed, (((1,), (1,)), ((), ())), preferred_element_type=jnp.float32
    )
    projected = lax.psum(partial_sums, "ch")
    step_low = projected[:RANK].astype(jnp.bfloat16)
    state_entry = projected[RANK : RANK + STATE]
    state_readout = projected[RANK + STATE :]
    step_raw = lax.dot_general(
        step_low, step_weight, (((0,), (0,)), ((), ())), preferred_element_type=jnp.float32
    )
    step_size = smooth_relu(step_raw + step_bias[None, :])
    decay_rate = -jnp.exp(decay_log)
    smoothed_wide = smoothed.astype(jnp.float32)

    def advance(loop_carry, inputs):
        state_now, elapsed = loop_carry
        size_now, value_now, entry_now, readout_now = inputs
        state_now = (
            jnp.exp(size_now[None, :] * decay_rate) * state_now
            + (size_now * value_now)[None, :] * entry_now[:, None]
        )
        elapsed = elapsed + size_now
        return ((state_now, elapsed), (jnp.sum(readout_now[:, None] * state_now, axis=0), elapsed))

    start_carry = (jnp.zeros((STATE, channels), jnp.float32), jnp.zeros((channels,), jnp.float32))
    final_carry, outputs = lax.scan(
        advance, start_carry, (step_size, smoothed_wide, state_entry.T, state_readout.T), unroll=16
    )
    local_state, elapsed_total = final_carry
    scanned, elapsed = outputs
    through = jnp.exp(decay_rate * elapsed_total[None, :])

    def relay_step(step_index, incoming):
        return from_behind(through * incoming + local_state, "ctx", 1)

    incoming = lax.fori_loop(0, lax.axis_size("ctx") - 1, relay_step, jnp.zeros_like(local_state))
    correction = jnp.zeros_like(scanned)
    for index_state in range(STATE):
        correction = (
            correction
            + state_readout[index_state][:, None]
            * jnp.exp(decay_rate[index_state][None, :] * elapsed)
            * incoming[index_state][None, :]
        )
    mixer_input = (
        (scanned + correction + skip_gain[None, :] * smoothed_wide)
        * sigmoid_linear(gate_input.astype(jnp.float32))
    ).astype(jnp.bfloat16)
    mixer_out = lax.psum(jnp.dot(mixer_input, out_weight, preferred_element_type=jnp.float32), "ch")
    stream = lax.all_gather(residual, "ch", axis=1, tiled=True)
    hidden = stream.astype(jnp.float32) + mixer_out
    normed = (
        hidden
        * lax.rsqrt(jnp.mean(hidden * hidden, axis=1, keepdims=True) + 1e-06)
        * norm_gain[None, :]
    ).astype(jnp.bfloat16)
    vocab_cols = head_weight.shape[1]
    logits = jnp.dot(
        normed,
        lax.all_gather(head_weight, "ctx", axis=0, tiled=True),
        preferred_element_type=jnp.float32,
    )
    column = lax.broadcasted_iota(jnp.int32, logits.shape, 1) + lax.axis_index("ch") * vocab_cols
    picked = jnp.sum(jnp.where(column == targets[:, None], logits, 0.0), axis=1)
    row_peak = lax.pmax(jnp.max(logits, axis=1), "ch")
    shifted = logits - row_peak[:, None]
    weights = jnp.exp(shifted)
    row_total, row_first, row_second, picked = lax.psum(
        (
            jnp.sum(weights, axis=1),
            jnp.sum(weights * shifted, axis=1),
            jnp.sum(weights * shifted * shifted, axis=1),
            picked,
        ),
        "ch",
    )
    log_total = jnp.log(row_total)
    mean_ratio = row_first / row_total
    return (
        picked - row_peak - log_total,
        mean_ratio - log_total,
        row_second / row_total - mean_ratio * mean_ratio,
    )


def solution(mesh):
    in_specs = (
        P("ctx", "ch"),
        P("ctx", "ch"),
        P(None, "ch"),
        P("ch"),
        P(None, "ch"),
        P(None, "ch"),
        P("ch"),
        P(None, "ch"),
        P("ch"),
        P("ch", None),
        P("ctx", "ch"),
        P(),
        P("ctx", "ch"),
        P("ctx"),
    )
    out_specs = (P("ctx"), P("ctx"), P("ctx"))
    return jax.shard_map(
        per_device, mesh=mesh, in_specs=in_specs, out_specs=out_specs, check_vma=False
    )
```

profile of v0, /device:TPU:8, one launch (start us, length us, event | category | flops | bytes accessed | tf_op | source)
XLA Modules:
  0.0 688.0 jit_solution(6019642598044573003)
XLA Ops:
  8.0 1.7 collective-permute-start.1
  14.0 1.7 convolution_bitcast_fusion
  17.2 2.5 convert.6
  19.7 98.2 %all-reduce.4.cloned.1.call-done = f32[544,384]{1,0:T(8,128)} async-done(((f32[544,384]{1,0:T(8,128)}), f32[544,384]{1,0:T(8,128)}) %all-reduce.4.cloned.1.call-update) | async-done | bytes 835600 | tf_op jit(solution)/shard_map/psum | solution.py:51
  118.9 3.9 compare_select_fusion
  122.8 116.6 %while.28 = (s32[]{:T(128)}, f32[16,1024]{1,0:T(8,128)S(1)}, f32[1024]{0:T(1024)S(1)}, f32[24,16,1024]{2,1,0:T(8,128)}, f32[24,16,1024]{2,1,0:T(8,128)}, /*index...) while((s32[]{:T(128)}, f32[16,1024]{1,0:T(8,128)S(1)}, ...), condition=%wide.region_18.19_spmd.clone, body=%wide.region_1.18_spmd.clone.sunk | while | flops 2343954 | bytes 2588525 | solution.py:73
  142.1 1.5 constant_dynamic-slice_fusion.66
  201.9 1.5 constant_dynamic-slice_fusion.67
  240.9 80.6 %while.27 = (s32[]{:T(128)}, f32[16,1024]{1,0:T(8,128)S(1)}, f32[16,1024]{1,0:T(8,128)S(1)}, f32[16,1024]{1,0:T(8,128)S(1)}, s32[]{:T(128)}) while((s32[]{:T(128)}, f32[16,1024]{1,0:T(8,128)S(1)}, f32[16,1024]{1,0:T(8,128)S(1)}, f32[16,1024]{1,0:T(8,128)S(1)}, s32[]{:T(128)}) %tuple.214), condition=%wide.region_20.21_spmd, body=%wide.region_19.20_spmd.sunk | while | flops 32770 | bytes 524389 | solution.py:83
  243.2 4.6 collective-permute-start
  248.7 4.7 collective-permute-start
  254.3 4.7 collective-permute-start
  259.9 4.7 collective-permute-start
  265.5 4.7 collective-permute-start
  271.1 4.7 collective-permute-start
  276.7 4.7 collective-permute-start
  282.3 4.7 collective-permute-start
  287.9 4.7 collective-permute-start
  293.5 4.7 collective-permute-start
  299.1 4.7 collective-permute-start
  304.7 4.7 collective-permute-start
  310.3 4.7 collective-permute-start
  315.9 4.7 collective-permute-start
  321.7 8.7 %fusion.111 = bf16[384,1024]{1,0:T(8,128)(2,1)S(1)} fusion(bf16[384,1024]{1,0:T(8,128)(2,1)} %param.19, f32[24,16,1024]{2,1,0:T(8,128)} %get-tuple-element.81, f32[24,16,1024]{2,1,0:T(8,128)} %get-tuple-element.80, f32[1024]{0:T(1024)S(1)} %copy-done.22, f32[1024]{0:T(1024)S(1)} %bitcast.639, f32[1024]{0:T(1024)S(1)} %bitcast.637, ...), kind=kLoop, calls=%fused_computation.241 | loop fusion | flops 33423360 | bytes 11190272 | tf_op jit(solution)/shard_map/convert_element_type | solution.py:95
  330.5 5.3 fusion.117
  336.4 153.1 %all-reduce.6.cloned.1.call-done = f32[384,4096]{1,0:T(8,128)} async-done(((f32[384,4096]{1,0:T(8,128)}), f32[384,4096]{1,0:T(8,128)}) %all-reduce.6.cloned.1.call-update) | async-done | bytes 6291472 | tf_op jit(solution)/shard_map/psum | solution.py:96
  489.5 4.6 multiply_reduce_fusion.16
  494.1 92.5 %all-gather.5.cloned.1.call-done = bf16[4096,2048]{1,0:T(8,128)(2,1)} async-done(((bf16[256,2048]{1,0:T(8,128)(2,1)}), bf16[4096,2048]{1,0:T(8,128)(2,1)}) %all-gather.5.cloned.1.call-update) | async-done | bytes 16777232 | tf_op jit(solution)/shard_map/all_gather | solution.py:107
  586.6 14.3 %fusion.116 = (f32[384]{0:T(512)S(1)}, f32[384,2048]{1,0:T(8,128)}) fusion(bf16[4096,2048]{1,0:T(8,128)(2,1)} %all-gather.5.cloned.1.call-done, f32[384,4096]{1,0:T(8,128)} %all-reduce.6.cloned.1.call-done, bf16[384,4096]{1,0:T(8,128)(2,1)} %all-gather.3.cloned.1.call-done, f32[4096]{0:T(1024)S(1)} %copy-done.20, f32[384]{0:T(512)S(1)} %add_rsqrt_fusion), kind=kOutput, calls=%fused_computation.274 | convolution fusion | flops 6451101184 | bytes 29379584 | tf_op jit(solution)/shard_map/dot_general | solution.py:105
  600.9 36.3 %pmax.7 = f32[384]{0:T(512)S(1)} all-reduce(f32[384]{0:T(512)S(1)} %get-tuple-element.335), channel_id=1, replica_groups=mesh['ctx'=16,'ch'=16] {'ch'}, use_global_device_ids=true, to_apply=%region_26.27 | all-reduce | flops 384 | bytes 3072 | tf_op jit(solution)/shard_map/pmax | solution.py:112
  637.2 3.2 fusion.35
  640.5 40.4 %all-reduce = (f32[384]{0:T(512)S(1)}, f32[384]{0:T(512)S(1)}, f32[384]{0:T(512)S(1)}, f32[384]{0:T(512)S(1)}) all-reduce(f32[384]{0:T(512)S(1)} %get-tuple-element.156, f32[384]{0:T(512)S(1)} %get-tuple-element.155, f32[384]{0:T(512)S(1)} %get-tuple-element.154, ...), channel_id=1, replica_groups=mesh['ctx'=16,'ch'=16] {'ch'}, use_global_device_ids=true, to_apply=%region_24.25 | all-reduce | flops 1536 | bytes 12288 | tf_op jit(solution)/shard_map/psum | solution.py:115
  (801 shorter events, 134.5 us)
Async XLA Ops:
  7.2 110.7 %all-reduce.4.cloned.1.call-start = ((), (), s32[]{:S(2)}) async-start(), calls=%async_computation.1 | async-start | bytes 1671168 | tf_op jit(solution)/shard_map/psum | solution.py:51
  8.0 2.6 collective-permute-start.1
  15.7 320.7 %all-gather.3.cloned.1.call-start = ((), (), s32[]{:S(2)}) async-start(), calls=%async_computation | async-start | bytes 3342336 | tf_op jit(solution)/shard_map/all_gather | solution.py:97
  16.4 473.1 %all-reduce.6.cloned.1.call-start = ((), (), s32[]{:S(2)}) async-start(), calls=%async_computation.2 | async-start | bytes 12582912 | tf_op jit(solution)/shard_map/psum | solution.py:96
  16.5 102.4 %copy-start.21 = (f32[1024]{0:T(1024)S(1)}, f32[1024]{0:T(1024)}, u32[]{:S(2)}) copy-start(f32[1024]{0:T(1024)} %param.24) | copy-start | bytes 12292
  239.5 82.1 %copy-start.5 = (f32[1,1024]{1,0:T(1,128)S(1)}, f32[1,1024]{1,0:T(1,128)}, u32[]{:S(2)}) copy-start(f32[1,1024]{1,0:T(1,128)} %get-tuple-element.299) | copy-start | bytes 12292
  239.5 82.1 %copy-start.6 = (f32[1,1024]{1,0:T(1,128)S(1)}, f32[1,1024]{1,0:T(1,128)}, u32[]{:S(2)}) copy-start(f32[1,1024]{1,0:T(1,128)} %get-tuple-element.300) | copy-start | bytes 12292
  239.5 82.1 %copy-start.7 = (f32[1,1024]{1,0:T(1,128)S(1)}, f32[1,1024]{1,0:T(1,128)}, u32[]{:S(2)}) copy-start(f32[1,1024]{1,0:T(1,128)} %get-tuple-element.301) | copy-start | bytes 12292
  239.5 82.1 %copy-start.8 = (f32[1,1024]{1,0:T(1,128)S(1)}, f32[1,1024]{1,0:T(1,128)}, u32[]{:S(2)}) copy-start(f32[1,1024]{1,0:T(1,128)} %get-tuple-element.302) | copy-start | bytes 12292
  239.5 82.1 %copy-start.9 = (f32[1,1024]{1,0:T(1,128)S(1)}, f32[1,1024]{1,0:T(1,128)}, u32[]{:S(2)}) copy-start(f32[1,1024]{1,0:T(1,128)} %get-tuple-element.303) | copy-start | bytes 12292
  239.5 82.1 %copy-start.10 = (f32[1,1024]{1,0:T(1,128)S(1)}, f32[1,1024]{1,0:T(1,128)}, u32[]{:S(2)}) copy-start(f32[1,1024]{1,0:T(1,128)} %get-tuple-element.304) | copy-start | bytes 12292
  239.5 82.1 %copy-start.11 = (f32[1,1024]{1,0:T(1,128)S(1)}, f32[1,1024]{1,0:T(1,128)}, u32[]{:S(2)}) copy-start(f32[1,1024]{1,0:T(1,128)} %get-tuple-element.305) | copy-start | bytes 12292
  239.5 82.1 %copy-start.12 = (f32[1,1024]{1,0:T(1,128)S(1)}, f32[1,1024]{1,0:T(1,128)}, u32[]{:S(2)}) copy-start(f32[1,1024]{1,0:T(1,128)} %get-tuple-element.306) | copy-start | bytes 12292
  239.5 82.1 %copy-start.13 = (f32[1,1024]{1,0:T(1,128)S(1)}, f32[1,1024]{1,0:T(1,128)}, u32[]{:S(2)}) copy-start(f32[1,1024]{1,0:T(1,128)} %get-tuple-element.307) | copy-start | bytes 12292
  241.0 2.2 collective-permute-start
  243.2 5.5 collective-permute-start
  248.7 5.6 collective-permute-start
  254.3 5.6 collective-permute-start
  259.9 5.6 collective-permute-start
  265.5 5.6 collective-permute-start
  271.1 5.6 collective-permute-start
  276.7 5.6 collective-permute-start
  282.3 5.6 collective-permute-start
  287.9 5.6 collective-permute-start
  293.5 5.6 collective-permute-start
  299.1 5.6 collective-permute-start
  304.7 5.6 collective-permute-start
  310.3 5.6 collective-permute-start
  315.9 5.6 collective-permute-start
  335.7 250.9 %all-gather.5.cloned.1.call-start = ((), (), s32[]{:S(2)}) async-start(), calls=%async_computation.3 | async-start | bytes 17825792 | tf_op jit(solution)/shard_map/all_gather | solution.py:107
  336.3 250.3 %copy-start.20 = (f32[4096]{0:T(1024)S(1)}, f32[4096]{0:T(1024)}, u32[]{:S(2)}) copy-start(f32[4096]{0:T(1024)} %param.29) | copy-start | bytes 49156
  494.1 143.1 %copy-start.18 = (s32[384]{0:T(512)S(1)}, s32[384]{0:T(512)}, u32[]{:S(2)}) copy-start(s32[384]{0:T(512)} %param.31) | copy-start | bytes 4612
  (11 other events, 516.4 us)
Sparse Core Ops, SparseCore 0:
  15.8 102.0 all-reduce.3
  120.3 56.3 all-gather.2
  335.9 153.5 all-reduce.5
  491.2 95.4 all-gather.4
where the time goes:
time: 694 us; the launch traced here: 688 us
  waiting for transfers between devices  358 us (52%)
  local copies, waits for them, and re-layouts  95.7 us (14%)
  blocking collectives  76.8 us (11%)
  starting transfers between devices  69 us (10%)
  other arithmetic  45 us (6%)
  matrix products  25.1 us (4%)
  between operations  14.2 us (2%)
    psum x1, waiting for transfers between devices, per_device(): lax.psum(jnp.dot(mixer_input, out_weight, preferred_element_type=jnp.floa...  153 us
    psum x1, waiting for transfers between devices, per_device(): projected = lax.psum(partial_sums, 'ch')  98.2 us
    all_gather x1, waiting for transfers between devices, per_device(): lax.all_gather(head_weight, 'ctx', axis=0, tiled=True)  92.5 us
    ppermute x16, starting transfers between devices, from_behind(): return lax.ppermute(shard, axis, pairs)  68.7 us
    slice x48, local copies, waits for them, and re-layouts, per_device(): lax.scan(advance, start_carry, (step_size, smoothed_wide, state_entry.T,...  63.6 us
    psum x1, blocking collectives, per_device(): lax.psum((jnp.sum(weights, axis=1), jnp.sum(weights * shifted, axis=1), j...  40.4 us
    pmax x1, blocking collectives, per_device(): row_peak = lax.pmax(jnp.max(logits, axis=1), 'ch')  36.3 us
    reduce_sum x120, other arithmetic, advance(): jnp.sum(readout_now[:, None] * state_now, axis=0)  19.8 us
  transfers between devices with their start and end apart: 20, of which 18 were waited for; matrix products, arithmetic and copies ran while one was open for 21% of the time, Pallas kernels for 0%

commit v1 on v0

--- a/solution.py
+++ b/solution.py
@@ -1,3 +1,4 @@
+import functools
 import jax
 import jax.numpy as jnp
 from jax import lax
@@ -6,6 +7,16 @@
 STATE = 16
 RANK = 512
 KCONV = 4
+
+
+def step_on_sites_up(vector, axis_key):
+    return jnp.concatenate(
+        lax.all_to_all(jnp.stack(lax.axis_size(axis_key) * [vector], axis=0), axis_key, 0, 0),
+        axis=0,
+    )
+
+
+_draft_cubes = functools.partial(step_on_sites_up, axis_key="ctx")
 
 
 def from_behind(shard, axis, by):
@@ -102,11 +113,7 @@
         * norm_gain[None, :]
     ).astype(jnp.bfloat16)
     vocab_cols = head_weight.shape[1]
-    logits = jnp.dot(
-        normed,
-        lax.all_gather(head_weight, "ctx", axis=0, tiled=True),
-        preferred_element_type=jnp.float32,
-    )
+    logits = jnp.dot(normed, _draft_cubes(head_weight), preferred_element_type=jnp.float32)
     column = lax.broadcasted_iota(jnp.int32, logits.shape, 1) + lax.axis_index("ch") * vocab_cols
     picked = jnp.sum(jnp.where(column == targets[:, None], logits, 0.0), axis=1)
     row_peak = lax.pmax(jnp.max(logits, axis=1), "ch")

time: 694 us -> 753 us (1.085)
  starting transfers between devices: 69 us -> 232 us
  waiting for transfers between devices: 358 us -> 247 us
    ppermute x16, starting transfers between devices: 68.7 us -> 220 us  [from_behind(): return lax.ppermute(shard, axis, pairs)]
    all_gather x1 -> x0, waiting for transfers between devices: 92.5 us -> none  [per_device(): lax.all_gather(head_weight, 'ctx', axis=0, tiled=True)]
    psum x1, waiting for transfers between devices: 98.2 us -> 80 us  [per_device(): projected = lax.psum(partial_sums, 'ch')]
    all_to_all x0 -> x1, starting transfers between devices: none -> 12.3 us  [step_on_sites_up(): lax.all_to_all(jnp.stack(lax.axis_size(axis_key) * [vector], axis=0), axi...]
  transfers between devices with their start and end apart: 20 -> 20, of which waited for: 18 -> 17; matrix products, arithmetic and copies ran while one was open for 21% -> 20% of each run, Pallas kernels for 0% -> 0%
where the time goes in v1:
time: 753 us; the launch traced here: 747 us
  waiting for transfers between devices  247 us (33%)
  starting transfers between devices  232 us (31%)
  local copies, waits for them, and re-layouts  102 us (14%)
  blocking collectives  75.1 us (10%)
  other arithmetic  43.7 us (6%)
  matrix products  28.5 us (4%)
  between operations  14.1 us (2%)
    ppermute x16, starting transfers between devices, from_behind(): return lax.ppermute(shard, axis, pairs)  220 us
    psum x1, waiting for transfers between devices, per_device(): lax.psum(jnp.dot(mixer_input, out_weight, preferred_element_type=jnp.floa...  154 us
    psum x1, waiting for transfers between devices, per_device(): projected = lax.psum(partial_sums, 'ch')  80 us
    slice x48, local copies, waits for them, and re-layouts, per_device(): lax.scan(advance, start_carry, (step_size, smoothed_wide, state_entry.T,...  65 us
    psum x1, blocking collectives, per_device(): lax.psum((jnp.sum(weights, axis=1), jnp.sum(weights * shifted, axis=1), j...  38.9 us
    pmax x1, blocking collectives, per_device(): row_peak = lax.pmax(jnp.max(logits, axis=1), 'ch')  36.2 us
    reduce_sum x120, other arithmetic, advance(): jnp.sum(readout_now[:, None] * state_now, axis=0)  19.7 us
    dynamic_update_slice x24, local copies, waits for them, and re-layouts, per_device(): lax.scan(advance, start_carry, (step_size, smoothed_wide, state_entry.T,...  15.8 us
  transfers between devices with their start and end apart: 20, of which 17 were waited for; matrix products, arithmetic and copies ran while one was open for 20% of the time, Pallas kernels for 0%

profile of v1, /device:TPU:8, one launch (start us, length us, event | category | flops | bytes accessed | tf_op | source)
XLA Modules:
  0.0 747.0 jit_solution(2910671968938132205)
XLA Ops:
  8.0 1.7 collective-permute-start.1
  13.1 1.7 convolution_bitcast_fusion
  14.8 6.9 stack.2
  21.7 12.3 %all-to-all-start = ((bf16[16,256,2048]{2,1,0:T(8,128)(2,1)}), bf16[16,256,2048]{2,1,0:T(8,128)(2,1)}, u32[]{:S(2)}, u32[]{:S(2)}) async-start(bf16[16,256,2048]{2,1,0:T(8,128)(2,1)} %stack.2), calls=%async_computation | async-start | bytes 33554432 | tf_op jit(solution)/shard_map/all_to_all | solution.py:14
  37.0 80.0 %all-reduce.4.cloned.1.call-done = f32[544,384]{1,0:T(8,128)} async-done(((f32[544,384]{1,0:T(8,128)}), f32[544,384]{1,0:T(8,128)}) %all-reduce.4.cloned.1.call-update) | async-done | bytes 835600 | tf_op jit(solution)/shard_map/psum | solution.py:62
  118.0 3.9 compare_select_fusion
  121.9 116.7 %while.28 = (s32[]{:T(128)}, f32[16,1024]{1,0:T(8,128)S(1)}, f32[1024]{0:T(1024)S(1)}, f32[24,16,1024]{2,1,0:T(8,128)}, f32[24,16,1024]{2,1,0:T(8,128)}, /*index...) while((s32[]{:T(128)}, f32[16,1024]{1,0:T(8,128)S(1)}, ...), condition=%wide.region_18.19_spmd.clone, body=%wide.region_1.18_spmd.clone.sunk | while | flops 2343954 | bytes 2588025 | solution.py:84
  194.7 1.6 constant_dynamic-slice_fusion.66
  210.8 1.6 constant_dynamic-slice_fusion.67
  239.9 231.5 %while.27 = (s32[]{:T(128)}, f32[16,1024]{1,0:T(8,128)S(1)}, f32[16,1024]{1,0:T(8,128)S(1)}, f32[16,1024]{1,0:T(8,128)S(1)}, s32[]{:T(128)}) while((s32[]{:T(128)}, f32[16,1024]{1,0:T(8,128)S(1)}, f32[16,1024]{1,0:T(8,128)S(1)}, f32[16,1024]{1,0:T(8,128)S(1)}, s32[]{:T(128)}) %tuple.214), condition=%wide.region_20.21_spmd, body=%wide.region_19.20_spmd.sunk | while | flops 32770 | bytes 524389 | solution.py:94
  242.1 155.5 %collective-permute-start = (f32[16,1024]{1,0:T(8,128)S(1)}, f32[16,1024]{1,0:T(8,128)S(1)}, u32[]{:S(2)}, u32[]{:S(2)}) collective-permute-start(f32[16,1024]{1,0:T(8,128)S(1)} %multiply_add_fusion.22), channel_id=1, source_target_pairs={{0,16},{16,32},{32,48},{48,64},{64,80},{80,96},{96,112},{112,128},... | collective-permute-start | bytes 196616 | tf_op jit(solution)/shard_map/while/body/eval_jaxpr/ppermute | solution.py:25
  398.5 4.8 collective-permute-start
  404.2 4.7 collective-permute-start
  409.9 4.7 collective-permute-start
  415.5 4.7 collective-permute-start
  421.1 4.7 collective-permute-start
  426.7 4.7 collective-permute-start
  432.3 4.7 collective-permute-start
  437.9 4.7 collective-permute-start
  443.5 4.7 collective-permute-start
  449.1 4.7 collective-permute-start
  454.7 4.7 collective-permute-start
  460.3 4.7 collective-permute-start
  465.9 4.7 collective-permute-start
  471.6 8.6 %fusion.111 = bf16[384,1024]{1,0:T(8,128)(2,1)S(1)} fusion(bf16[384,1024]{1,0:T(8,128)(2,1)} %param.19, f32[24,16,1024]{2,1,0:T(8,128)} %get-tuple-element.81, f32[24,16,1024]{2,1,0:T(8,128)} %get-tuple-element.80, f32[1024]{0:T(1024)S(1)} %copy-done.17, f32[1024]{0:T(1024)S(1)} %bitcast.640, f32[1024]{0:T(1024)S(1)} %bitcast.638, ...), kind=kLoop, calls=%fused_computation.241 | loop fusion | flops 33423360 | bytes 11190272 | tf_op jit(solution)/shard_map/convert_element_type | solution.py:106
  480.2 8.6 %fusion.117 = f32[384,4096]{1,0:T(8,128)} fusion(bf16[384,1024]{1,0:T(8,128)(2,1)S(1)} %fusion.111, bf16[1024,4096]{1,0:T(8,128)(2,1)} %param.27), kind=kOutput, calls=%fused_computation.275 | convolution fusion | flops 3221225472 | bytes 15466496 | tf_op jit(solution)/shard_map/dot_general | solution.py:107
  488.9 153.6 %all-reduce.6.cloned.1.call-done = f32[384,4096]{1,0:T(8,128)} async-done(((f32[384,4096]{1,0:T(8,128)}), f32[384,4096]{1,0:T(8,128)}) %all-reduce.6.cloned.1.call-update) | async-done | bytes 6291472 | tf_op jit(solution)/shard_map/psum | solution.py:107
  642.5 4.6 multiply_reduce_fusion.16
  647.1 14.3 %fusion.116 = (f32[384]{0:T(512)S(1)}, f32[384,2048]{1,0:T(8,128)}) fusion(bf16[4096,2048]{1,0:T(8,128)(2,1)} %bitcast.45, f32[384,4096]{1,0:T(8,128)} %all-reduce.6.cloned.1.call-done, bf16[384,4096]{1,0:T(8,128)(2,1)} %all-gather.2.cloned.1.call-done, f32[4096]{0:T(1024)S(1)} %copy-done.15, f32[384]{0:T(512)S(1)} %add_rsqrt_fusion), kind=kOutput, calls=%fused_computation.274 | convolution fusion | flops 6451101184 | bytes 29379584 | tf_op jit(solution)/shard_map/dot_general | solution.py:116
  661.4 36.2 %pmax.7 = f32[384]{0:T(512)S(1)} all-reduce(f32[384]{0:T(512)S(1)} %get-tuple-element.335), channel_id=1, replica_groups=mesh['ctx'=16,'ch'=16] {'ch'}, use_global_device_ids=true, to_apply=%region_26.27 | all-reduce | flops 384 | bytes 3072 | tf_op jit(solution)/shard_map/pmax | solution.py:119
  697.6 3.3 fusion.35
  700.9 38.9 %all-reduce = (f32[384]{0:T(512)S(1)}, f32[384]{0:T(512)S(1)}, f32[384]{0:T(512)S(1)}, f32[384]{0:T(512)S(1)}) all-reduce(f32[384]{0:T(512)S(1)} %get-tuple-element.156, f32[384]{0:T(512)S(1)} %get-tuple-element.155, f32[384]{0:T(512)S(1)} %get-tuple-element.154, ...), channel_id=1, replica_groups=mesh['ctx'=16,'ch'=16] {'ch'}, use_global_device_ids=true, to_apply=%region_24.25 | all-reduce | flops 1536 | bytes 12288 | tf_op jit(solution)/shard_map/psum | solution.py:122
  (791 shorter events, 134.3 us)
Async XLA Ops:
  7.2 109.8 %all-reduce.4.cloned.1.call-start = ((), (), s32[]{:S(2)}) async-start(), calls=%async_computation.2 | async-start | bytes 1671168 | tf_op jit(solution)/shard_map/psum | solution.py:62
  8.0 2.6 collective-permute-start.1
  21.7 625.4 %all-to-all-start = ((bf16[16,256,2048]{2,1,0:T(8,128)(2,1)}), bf16[16,256,2048]{2,1,0:T(8,128)(2,1)}, u32[]{:S(2)}, u32[]{:S(2)}) async-start(bf16[16,256,2048]{2,1,0:T(8,128)(2,1)} %stack.2), calls=%async_computation | async-start | bytes 33554432 | tf_op jit(solution)/shard_map/all_to_all | solution.py:14
  34.0 454.9 %all-gather.2.cloned.1.call-start = ((), (), s32[]{:S(2)}) async-start(), calls=%async_computation.1 | async-start | bytes 3342336 | tf_op jit(solution)/shard_map/all_gather | solution.py:108
  34.7 607.7 %all-reduce.6.cloned.1.call-start = ((), (), s32[]{:S(2)}) async-start(), calls=%async_computation.3 | async-start | bytes 12582912 | tf_op jit(solution)/shard_map/psum | solution.py:107
  121.9 118.0 %copy-start.3 = (f32[16,1024]{1,0:T(8,128)S(1)}, f32[16,1024]{1,0:T(8,128)}, u32[]{:S(2)}) copy-start(f32[16,1024]{1,0:T(8,128)} %param.25) | copy-start | bytes 196612
  238.6 233.0 %copy-start.5 = (f32[1,1024]{1,0:T(1,128)S(1)}, f32[1,1024]{1,0:T(1,128)}, u32[]{:S(2)}) copy-start(f32[1,1024]{1,0:T(1,128)} %get-tuple-element.303) | copy-start | bytes 12292
  238.6 233.0 %copy-start.6 = (f32[1,1024]{1,0:T(1,128)S(1)}, f32[1,1024]{1,0:T(1,128)}, u32[]{:S(2)}) copy-start(f32[1,1024]{1,0:T(1,128)} %get-tuple-element.304) | copy-start | bytes 12292
  238.6 233.0 %copy-start.7 = (f32[1,1024]{1,0:T(1,128)S(1)}, f32[1,1024]{1,0:T(1,128)}, u32[]{:S(2)}) copy-start(f32[1,1024]{1,0:T(1,128)} %get-tuple-element.305) | copy-start | bytes 12292
  238.6 233.0 %copy-start.8 = (f32[1,1024]{1,0:T(1,128)S(1)}, f32[1,1024]{1,0:T(1,128)}, u32[]{:S(2)}) copy-start(f32[1,1024]{1,0:T(1,128)} %get-tuple-element.306) | copy-start | bytes 12292
  238.6 233.0 %copy-start.9 = (f32[1,1024]{1,0:T(1,128)S(1)}, f32[1,1024]{1,0:T(1,128)}, u32[]{:S(2)}) copy-start(f32[1,1024]{1,0:T(1,128)} %get-tuple-element.307) | copy-start | bytes 12292
  238.6 233.0 %copy-start.10 = (f32[1,1024]{1,0:T(1,128)S(1)}, f32[1,1024]{1,0:T(1,128)}, u32[]{:S(2)}) copy-start(f32[1,1024]{1,0:T(1,128)} %get-tuple-element.308) | copy-start | bytes 12292
  238.6 233.0 %copy-start.11 = (f32[1,1024]{1,0:T(1,128)S(1)}, f32[1,1024]{1,0:T(1,128)}, u32[]{:S(2)}) copy-start(f32[1,1024]{1,0:T(1,128)} %get-tuple-element.309) | copy-start | bytes 12292
  238.6 233.0 %copy-start.12 = (f32[1,1024]{1,0:T(1,128)S(1)}, f32[1,1024]{1,0:T(1,128)}, u32[]{:S(2)}) copy-start(f32[1,1024]{1,0:T(1,128)} %get-tuple-element.310) | copy-start | bytes 12292
  238.6 233.0 %copy-start.13 = (f32[1,1024]{1,0:T(1,128)S(1)}, f32[1,1024]{1,0:T(1,128)}, u32[]{:S(2)}) copy-start(f32[1,1024]{1,0:T(1,128)} %get-tuple-element.311) | copy-start | bytes 12292
  238.6 233.0 %copy-start.17 = (f32[1024]{0:T(1024)S(1)}, f32[1024]{0:T(1024)}, u32[]{:S(2)}) copy-start(f32[1024]{0:T(1024)} %param.26) | copy-start | bytes 12292
  239.9 2.2 collective-permute-start
  242.1 156.4 %collective-permute-start = (f32[16,1024]{1,0:T(8,128)S(1)}, f32[16,1024]{1,0:T(8,128)S(1)}, u32[]{:S(2)}, u32[]{:S(2)}) collective-permute-start(f32[16,1024]{1,0:T(8,128)S(1)} %multiply_add_fusion.22), channel_id=1, source_target_pairs={{0,16},{16,32},{32,48},{48,64},{64,80},{80,96},{96,112},{112,128},... | collective-permute-start | bytes 196616 | tf_op jit(solution)/shard_map/while/body/eval_jaxpr/ppermute | solution.py:25
  398.5 5.7 collective-permute-start
  404.2 5.6 collective-permute-start
  409.9 5.6 collective-permute-start
  415.5 5.6 collective-permute-start
  421.1 5.6 collective-permute-start
  426.7 5.6 collective-permute-start
  432.3 5.6 collective-permute-start
  437.9 5.6 collective-permute-start
  443.5 5.6 collective-permute-start
  449.1 5.6 collective-permute-start
  454.7 5.6 collective-permute-start
  460.3 5.6 collective-permute-start
  465.9 5.6 collective-permute-start
  488.8 158.3 %copy-start.15 = (f32[4096]{0:T(1024)S(1)}, f32[4096]{0:T(1024)}, u32[]{:S(2)}) copy-start(f32[4096]{0:T(1024)} %param.29) | copy-start | bytes 49156
  (6 other events, 200.4 us)
Sparse Core Ops, SparseCore 0:
  14.9 101.9 all-reduce.3
  119.4 56.4 all-gather.1
  488.9 153.4 all-reduce.5
